TPU v7x, 128 devices: a whole 4x4x4 slice. The times are simulated.
128 devices in a mesh: blk: 16 (over x_lo, y, core), head: 8 (over x_hi, z).
Axes of the slice: x: 4 (x_hi: 2, x_lo: 2; x = x_hi * 2 + x_lo), y: 4, z: 4, core: 2. Of those that a mesh axis runs over, the one named last changes fastest.
Arguments:
- queries: bfloat16 [16384, 3072], P(('blk', 'head')), may hold values from -100 to 100
- keys: bfloat16 [16384, 3072], P(('blk', 'head')), may hold values from -100 to 100
- values: bfloat16 [16384, 3072], P(('blk', 'head')), may hold values from -6 to 6
- query_gain: float32 [3072], replicated, may hold values from 1 to 4
- key_gain: float32 [3072], replicated, may hold values from 0.1 to 1.9
Outputs:
- attended: bfloat16 [16384, 3072], P(('blk', 'head'))
All inputs are finite; a program needn't handle non-finite values.
Results may differ from a plain program's by a relative error of at most 0.0075.
The roundings to bfloat16 on the way count: a program that leaves them out, or rounds other values in their place, can miss the bound.
Values may be sent and summed in bfloat16 or wider, within the bound.
A program may use at most 128 MiB of HBM per device.

v0:
```python
import math

import jax
import jax.numpy as jnp
from jax import lax
from jax.sharding import PartitionSpec as P

HEAD_DIM = 128


def normalize(block, gain):
    wide = block.astype(jnp.float32)
    mean_sq = jnp.mean(wide * wide, axis=-1, keepdims=True)
    return (wide * lax.rsqrt(mean_sq + 1e-06) * gain).astype(jnp.bfloat16)


def absorb(carry, pieces, q_heads, factor):
    run_max, run_sum, accum = carry
    key_block, value_block = pieces
    scores = (
        jnp.einsum("qhd,khd->hqk", q_heads, key_block, preferred_element_type=jnp.float32) * factor
    )
    new_max = jnp.maximum(run_max, jnp.max(scores, axis=-1))
    shrink = jnp.exp(run_max - new_max)
    weights = jnp.exp(scores - new_max[:, :, None])
    new_sum = run_sum * shrink + jnp.sum(weights, axis=-1)
    mixed = jnp.einsum(
        "hqk,khd->hqd",
        weights.astype(jnp.bfloat16),
        value_block,
        preferred_element_type=jnp.float32,
    )
    return (new_max, new_sum, accum * shrink[:, :, None] + mixed)


def shards(queries, keys, values, query_gain, key_gain):
    group = lax.axis_size("head")
    width = queries.shape[1] // group
    heads_here = width // HEAD_DIM
    factor = 1.0 / math.sqrt(HEAD_DIM)
    first_part = normalize(queries, query_gain)
    second_part = normalize(keys, key_gain)
    q_local, k_local, v_local = (
        lax.all_to_all(first_part, "head", split_axis=1, concat_axis=0, tiled=True),
        lax.all_to_all(second_part, "head", split_axis=1, concat_axis=0, tiled=True),
        lax.all_to_all(values, "head", split_axis=1, concat_axis=0, tiled=True),
    )
    rows = q_local.shape[0]
    q_heads = q_local.reshape(rows, heads_here, HEAD_DIM)
    k_heads = k_local.reshape(rows, heads_here, HEAD_DIM)
    v_heads = v_local.reshape(rows, heads_here, HEAD_DIM)
    start_state = (
        jnp.full((heads_here, rows), -jnp.inf, jnp.float32),
        jnp.zeros((heads_here, rows), jnp.float32),
        jnp.zeros((heads_here, rows, HEAD_DIM), jnp.float32),
    )
    key_piece = lax.all_gather(k_heads, "blk", axis=0, tiled=True)
    value_piece = lax.all_gather(v_heads, "blk", axis=0, tiled=True)
    length = key_piece.shape[0]
    block_rows = math.gcd(length, 1024)
    count = length // block_rows
    key_blocks = key_piece.reshape(count, block_rows, heads_here, HEAD_DIM)
    value_blocks = value_piece.reshape(count, block_rows, heads_here, HEAD_DIM)

    def step_fn(state, blocks):
        return (absorb(state, blocks, q_heads, factor), None)

    final_state, unused = lax.scan(step_fn, start_state, (key_blocks, value_blocks))
    run_max, run_sum, accum = final_state
    result = accum / run_sum[:, :, None]
    result = jnp.transpose(result, (1, 0, 2)).reshape(rows, width).astype(jnp.bfloat16)
    return lax.all_to_all(result, "head", split_axis=0, concat_axis=1, tiled=True)


def solution(mesh):
    placed = (
        P(("blk", "head"), None),
        P(("blk", "head"), None),
        P(("blk", "head"), None),
        P(),
        P(),
    )
    return jax.shard_map(
        shards, mesh=mesh, in_specs=placed, out_specs=P(("blk", "head"), None), check_vma=False
    )
```

profile of v0, /device:TPU:0, one launch (start us, length us, event | category | flops | bytes accessed | tf_op | source)
XLA Modules:
  0.0 578.3 jit_solution(14939098089677855722)
XLA Ops:
  6.5 1.4 fusion.19
  7.9 1.4 fusion.21
  9.7 22.0 %all_to_all.64 = bf16[128,8,384]{0,2,1:T(8,128)(2,1)S(1)} all-to-all(bf16[128,8,384]{0,2,1:T(8,128)(2,1)S(1)} %bitcast.64), channel_id=1, replica_groups=mesh['blk'=16,'head'=8] {'head'}, dimensions={1} | all-to-all | bytes 1572864 | tf_op jit(solution)/shard_map/all_to_all | solution.py:45
  33.9 21.0 %all_to_all.65 = bf16[128,8,384]{0,2,1:T(8,128)(2,1)S(1)} all-to-all(bf16[128,8,384]{0,2,1:T(8,128)(2,1)S(1)} %bitcast.70), channel_id=1, replica_groups=mesh['blk'=16,'head'=8] {'head'}, dimensions={1} | all-to-all | bytes 1572864 | tf_op jit(solution)/shard_map/all_to_all | solution.py:46
  58.4 3.7 all-to-all-start.1
  62.2 18.7 %all-to-all-done.1 = bf16[128,8,384]{0,2,1:T(8,128)(2,1)S(1)} async-done(((bf16[128,8,384]{0,2,1:T(8,128)(2,1)}), bf16[128,8,384]{0,2,1:T(8,128)(2,1)S(1)}, u32[]{:S(2)}, u32[]{:S(2)}) %all-to-all-start.1) | async-done | bytes 786464 | tf_op jit(solution)/shard_map/all_to_all | solution.py:44
  82.8 31.2 %all-gather.3.cloned.1.call-done = bf16[16384,3,128]{0,2,1:T(8,128)(2,1)} async-done(((bf16[1024,3,128]{0,2,1:T(8,128)(2,1)}), bf16[16384,3,128]{0,2,1:T(8,128)(2,1)}) %all-gather.3.cloned.1.call-update) | async-done | bytes 12582928 | tf_op jit(solution)/shard_map/all_gather | solution.py:57
  114.0 16.7 %copy.32 = bf16[16384,3,128]{2,0,1:T(8,128)(2,1)} copy(bf16[16384,3,128]{0,2,1:T(8,128)(2,1)} %all-gather.3.cloned.1.call-done) | data formatting | bytes 25165824 | tf_op jit(solution)/shard_map/all_gather | solution.py:57
  130.7 59.0 %all-gather.5.cloned.1.call-done = bf16[16384,3,128]{0,2,1:T(8,128)(2,1)} async-done(((bf16[1024,3,128]{0,2,1:T(8,128)(2,1)}), bf16[16384,3,128]{0,2,1:T(8,128)(2,1)}) %all-gather.5.cloned.1.call-update) | async-done | bytes 12582928 | tf_op jit(solution)/shard_map/all_gather | solution.py:58
  189.6 16.6 %copy.37 = bf16[16384,3,128]{2,0,1:T(8,128)(2,1)} copy(bf16[16384,3,128]{0,2,1:T(8,128)(2,1)} %all-gather.5.cloned.1.call-done) | data formatting | bytes 25165824 | tf_op jit(solution)/shard_map/all_gather | solution.py:58
  206.2 340.2 %while.15 = (s32[]{:T(128)}, f32[3,1024]{1,0:T(4,128)S(1)}, f32[3,1024]{1,0:T(4,128)S(1)}, f32[3,1024,128]{2,1,0:T(8,128)}, bf16[16,1024,3,128]{3,1,0,2:T(8,128)...) while((s32[]{:T(128)}, f32[3,1024]{1,0:T(4,128)S(1)}, ...), condition=%wide.region_5.6_spmd.clone, body=%wide.region_2.5_spmd.clone.sunk | while | flops 1636973568 | bytes 93783168 | solution.py:68
  206.2 7.8 %bitcast_reduce_fusion.2 = (f32[3,1024]{1,0:T(4,128)S(1)}, f32[3,1024,1024]{2,1,0:T(8,128)}) fusion(bf16[1024,3,128]{2,0,1:T(8,128)(2,1)} %get-tuple-element.182, bf16[16,1024,3,128]{3,1,0,2:T(8,128)(2,1)} %get-tuple-element.181, s32[]{:T(128)} %get-tuple-element.168), kind=kOutput, calls=%fused_computation.1.clone.1 | convolution fusion | flops 811594752 | bytes 14168576 | tf_op jit(solution)/shard_map/while/body/eval_jaxpr/qhd,khd->hqk/dot_general | solution.py:21
  214.0 6.8 %fusion.36 = f32[3,1024]{1,0:T(4,128)S(1)} fusion(f32[3,1024,1024]{2,1,0:T(8,128)} %get-tuple-element.156, f32[3,1024]{1,0:T(4,128)S(1)} %select_maximum_fusion.2), kind=kLoop, calls=%fused_computation.4.clone.1 | loop fusion | flops 9434112 | bytes 12607488 | tf_op jit(solution)/shard_map/while/body/eval_jaxpr/reduce_sum | solution.py:26
  220.8 1.3 copy-done
  222.1 5.1 fusion.38
  227.3 7.8 %bitcast_reduce_fusion.2 = (f32[3,1024]{1,0:T(4,128)S(1)}, f32[3,1024,1024]{2,1,0:T(8,128)}) fusion(bf16[1024,3,128]{2,0,1:T(8,128)(2,1)} %get-tuple-element.182, bf16[16,1024,3,128]{3,1,0,2:T(8,128)(2,1)} %get-tuple-element.181, s32[]{:T(128)} %get-tuple-element.168), kind=kOutput, calls=%fused_computation.1.clone.1 | convolution fusion | flops 811594752 | bytes 14168576 | tf_op jit(solution)/shard_map/while/body/eval_jaxpr/qhd,khd->hqk/dot_general | solution.py:21
  235.0 6.8 %fusion.36 = f32[3,1024]{1,0:T(4,128)S(1)} fusion(f32[3,1024,1024]{2,1,0:T(8,128)} %get-tuple-element.156, f32[3,1024]{1,0:T(4,128)S(1)} %select_maximum_fusion.2), kind=kLoop, calls=%fused_computation.4.clone.1 | loop fusion | flops 9434112 | bytes 12607488 | tf_op jit(solution)/shard_map/while/body/eval_jaxpr/reduce_sum | solution.py:26
  241.8 1.3 copy-done
  243.2 5.4 fusion.38
  248.5 7.8 %bitcast_reduce_fusion.2 = (f32[3,1024]{1,0:T(4,128)S(1)}, f32[3,1024,1024]{2,1,0:T(8,128)}) fusion(bf16[1024,3,128]{2,0,1:T(8,128)(2,1)} %get-tuple-element.182, bf16[16,1024,3,128]{3,1,0,2:T(8,128)(2,1)} %get-tuple-element.181, s32[]{:T(128)} %get-tuple-element.168), kind=kOutput, calls=%fused_computation.1.clone.1 | convolution fusion | flops 811594752 | bytes 14168576 | tf_op jit(solution)/shard_map/while/body/eval_jaxpr/qhd,khd->hqk/dot_general | solution.py:21
  256.3 6.8 %fusion.36 = f32[3,1024]{1,0:T(4,128)S(1)} fusion(f32[3,1024,1024]{2,1,0:T(8,128)} %get-tuple-element.156, f32[3,1024]{1,0:T(4,128)S(1)} %select_maximum_fusion.2), kind=kLoop, calls=%fused_computation.4.clone.1 | loop fusion | flops 9434112 | bytes 12607488 | tf_op jit(solution)/shard_map/while/body/eval_jaxpr/reduce_sum | solution.py:26
  263.1 1.3 copy-done
  264.4 5.4 fusion.38
  269.8 7.8 %bitcast_reduce_fusion.2 = (f32[3,1024]{1,0:T(4,128)S(1)}, f32[3,1024,1024]{2,1,0:T(8,128)}) fusion(bf16[1024,3,128]{2,0,1:T(8,128)(2,1)} %get-tuple-element.182, bf16[16,1024,3,128]{3,1,0,2:T(8,128)(2,1)} %get-tuple-element.181, s32[]{:T(128)} %get-tuple-element.168), kind=kOutput, calls=%fused_computation.1.clone.1 | convolution fusion | flops 811594752 | bytes 14168576 | tf_op jit(solution)/shard_map/while/body/eval_jaxpr/qhd,khd->hqk/dot_general | solution.py:21
  277.6 6.8 %fusion.36 = f32[3,1024]{1,0:T(4,128)S(1)} fusion(f32[3,1024,1024]{2,1,0:T(8,128)} %get-tuple-element.156, f32[3,1024]{1,0:T(4,128)S(1)} %select_maximum_fusion.2), kind=kLoop, calls=%fused_computation.4.clone.1 | loop fusion | flops 9434112 | bytes 12607488 | tf_op jit(solution)/shard_map/while/body/eval_jaxpr/reduce_sum | solution.py:26
  285.7 5.4 fusion.38
  291.1 7.8 %bitcast_reduce_fusion.2 = (f32[3,1024]{1,0:T(4,128)S(1)}, f32[3,1024,1024]{2,1,0:T(8,128)}) fusion(bf16[1024,3,128]{2,0,1:T(8,128)(2,1)} %get-tuple-element.182, bf16[16,1024,3,128]{3,1,0,2:T(8,128)(2,1)} %get-tuple-element.181, s32[]{:T(128)} %get-tuple-element.168), kind=kOutput, calls=%fused_computation.1.clone.1 | convolution fusion | flops 811594752 | bytes 14168576 | tf_op jit(solution)/shard_map/while/body/eval_jaxpr/qhd,khd->hqk/dot_general | solution.py:21
  298.9 6.8 %fusion.36 = f32[3,1024]{1,0:T(4,128)S(1)} fusion(f32[3,1024,1024]{2,1,0:T(8,128)} %get-tuple-element.156, f32[3,1024]{1,0:T(4,128)S(1)} %select_maximum_fusion.2), kind=kLoop, calls=%fused_computation.4.clone.1 | loop fusion | flops 9434112 | bytes 12607488 | tf_op jit(solution)/shard_map/while/body/eval_jaxpr/reduce_sum | solution.py:26
  307.0 5.4 fusion.38
  312.4 7.8 %bitcast_reduce_fusion.2 = (f32[3,1024]{1,0:T(4,128)S(1)}, f32[3,1024,1024]{2,1,0:T(8,128)}) fusion(bf16[1024,3,128]{2,0,1:T(8,128)(2,1)} %get-tuple-element.182, bf16[16,1024,3,128]{3,1,0,2:T(8,128)(2,1)} %get-tuple-element.181, s32[]{:T(128)} %get-tuple-element.168), kind=kOutput, calls=%fused_computation.1.clone.1 | convolution fusion | flops 811594752 | bytes 14168576 | tf_op jit(solution)/shard_map/while/body/eval_jaxpr/qhd,khd->hqk/dot_general | solution.py:21
  320.1 6.8 %fusion.36 = f32[3,1024]{1,0:T(4,128)S(1)} fusion(f32[3,1024,1024]{2,1,0:T(8,128)} %get-tuple-element.156, f32[3,1024]{1,0:T(4,128)S(1)} %select_maximum_fusion.2), kind=kLoop, calls=%fused_computation.4.clone.1 | loop fusion | flops 9434112 | bytes 12607488 | tf_op jit(solution)/shard_map/while/body/eval_jaxpr/reduce_sum | solution.py:26
  328.3 5.4 fusion.38
  333.7 7.8 %bitcast_reduce_fusion.2 = (f32[3,1024]{1,0:T(4,128)S(1)}, f32[3,1024,1024]{2,1,0:T(8,128)}) fusion(bf16[1024,3,128]{2,0,1:T(8,128)(2,1)} %get-tuple-element.182, bf16[16,1024,3,128]{3,1,0,2:T(8,128)(2,1)} %get-tuple-element.181, s32[]{:T(128)} %get-tuple-element.168), kind=kOutput, calls=%fused_computation.1.clone.1 | convolution fusion | flops 811594752 | bytes 14168576 | tf_op jit(solution)/shard_map/while/body/eval_jaxpr/qhd,khd->hqk/dot_general | solution.py:21
  341.4 6.8 %fusion.36 = f32[3,1024]{1,0:T(4,128)S(1)} fusion(f32[3,1024,1024]{2,1,0:T(8,128)} %get-tuple-element.156, f32[3,1024]{1,0:T(4,128)S(1)} %select_maximum_fusion.2), kind=kLoop, calls=%fused_computation.4.clone.1 | loop fusion | flops 9434112 | bytes 12607488 | tf_op jit(solution)/shard_map/while/body/eval_jaxpr/reduce_sum | solution.py:26
  349.6 5.4 fusion.38
  354.9 7.8 %bitcast_reduce_fusion.2 = (f32[3,1024]{1,0:T(4,128)S(1)}, f32[3,1024,1024]{2,1,0:T(8,128)}) fusion(bf16[1024,3,128]{2,0,1:T(8,128)(2,1)} %get-tuple-element.182, bf16[16,1024,3,128]{3,1,0,2:T(8,128)(2,1)} %get-tuple-element.181, s32[]{:T(128)} %get-tuple-element.168), kind=kOutput, calls=%fused_computation.1.clone.1 | convolution fusion | flops 811594752 | bytes 14168576 | tf_op jit(solution)/shard_map/while/body/eval_jaxpr/qhd,khd->hqk/dot_general | solution.py:21
  362.7 6.8 %fusion.36 = f32[3,1024]{1,0:T(4,128)S(1)} fusion(f32[3,1024,1024]{2,1,0:T(8,128)} %get-tuple-element.156, f32[3,1024]{1,0:T(4,128)S(1)} %select_maximum_fusion.2), kind=kLoop, calls=%fused_computation.4.clone.1 | loop fusion | flops 9434112 | bytes 12607488 | tf_op jit(solution)/shard_map/while/body/eval_jaxpr/reduce_sum | solution.py:26
  370.8 5.4 fusion.38
  376.2 7.8 %bitcast_reduce_fusion.2 = (f32[3,1024]{1,0:T(4,128)S(1)}, f32[3,1024,1024]{2,1,0:T(8,128)}) fusion(bf16[1024,3,128]{2,0,1:T(8,128)(2,1)} %get-tuple-element.182, bf16[16,1024,3,128]{3,1,0,2:T(8,128)(2,1)} %get-tuple-element.181, s32[]{:T(128)} %get-tuple-element.168), kind=kOutput, calls=%fused_computation.1.clone.1 | convolution fusion | flops 811594752 | bytes 14168576 | tf_op jit(solution)/shard_map/while/body/eval_jaxpr/qhd,khd->hqk/dot_general | solution.py:21
  384.0 6.8 %fusion.36 = f32[3,1024]{1,0:T(4,128)S(1)} fusion(f32[3,1024,1024]{2,1,0:T(8,128)} %get-tuple-element.156, f32[3,1024]{1,0:T(4,128)S(1)} %select_maximum_fusion.2), kind=kLoop, calls=%fused_computation.4.clone.1 | loop fusion | flops 9434112 | bytes 12607488 | tf_op jit(solution)/shard_map/while/body/eval_jaxpr/reduce_sum | solution.py:26
  392.1 5.4 fusion.38
  397.5 7.8 %bitcast_reduce_fusion.2 = (f32[3,1024]{1,0:T(4,128)S(1)}, f32[3,1024,1024]{2,1,0:T(8,128)}) fusion(bf16[1024,3,128]{2,0,1:T(8,128)(2,1)} %get-tuple-element.182, bf16[16,1024,3,128]{3,1,0,2:T(8,128)(2,1)} %get-tuple-element.181, s32[]{:T(128)} %get-tuple-element.168), kind=kOutput, calls=%fused_computation.1.clone.1 | convolution fusion | flops 811594752 | bytes 14168576 | tf_op jit(solution)/shard_map/while/body/eval_jaxpr/qhd,khd->hqk/dot_general | solution.py:21
  405.3 6.8 %fusion.36 = f32[3,1024]{1,0:T(4,128)S(1)} fusion(f32[3,1024,1024]{2,1,0:T(8,128)} %get-tuple-element.156, f32[3,1024]{1,0:T(4,128)S(1)} %select_maximum_fusion.2), kind=kLoop, calls=%fused_computation.4.clone.1 | loop fusion | flops 9434112 | bytes 12607488 | tf_op jit(solution)/shard_map/while/body/eval_jaxpr/reduce_sum | solution.py:26
  413.4 5.4 fusion.38
  418.8 7.8 %bitcast_reduce_fusion.2 = (f32[3,1024]{1,0:T(4,128)S(1)}, f32[3,1024,1024]{2,1,0:T(8,128)}) fusion(bf16[1024,3,128]{2,0,1:T(8,128)(2,1)} %get-tuple-element.182, bf16[16,1024,3,128]{3,1,0,2:T(8,128)(2,1)} %get-tuple-element.181, s32[]{:T(128)} %get-tuple-element.168), kind=kOutput, calls=%fused_computation.1.clone.1 | convolution fusion | flops 811594752 | bytes 14168576 | tf_op jit(solution)/shard_map/while/body/eval_jaxpr/qhd,khd->hqk/dot_general | solution.py:21
  426.5 6.8 %fusion.36 = f32[3,1024]{1,0:T(4,128)S(1)} fusion(f32[3,1024,1024]{2,1,0:T(8,128)} %get-tuple-element.156, f32[3,1024]{1,0:T(4,128)S(1)} %select_maximum_fusion.2), kind=kLoop, calls=%fused_computation.4.clone.1 | loop fusion | flops 9434112 | bytes 12607488 | tf_op jit(solution)/shard_map/while/body/eval_jaxpr/reduce_sum | solution.py:26
  434.7 5.4 fusion.38
  440.1 7.8 %bitcast_reduce_fusion.2 = (f32[3,1024]{1,0:T(4,128)S(1)}, f32[3,1024,1024]{2,1,0:T(8,128)}) fusion(bf16[1024,3,128]{2,0,1:T(8,128)(2,1)} %get-tuple-element.182, bf16[16,1024,3,128]{3,1,0,2:T(8,128)(2,1)} %get-tuple-element.181, s32[]{:T(128)} %get-tuple-element.168), kind=kOutput, calls=%fused_computation.1.clone.1 | convolution fusion | flops 811594752 | bytes 14168576 | tf_op jit(solution)/shard_map/while/body/eval_jaxpr/qhd,khd->hqk/dot_general | solution.py:21
  447.8 6.8 %fusion.36 = f32[3,1024]{1,0:T(4,128)S(1)} fusion(f32[3,1024,1024]{2,1,0:T(8,128)} %get-tuple-element.156, f32[3,1024]{1,0:T(4,128)S(1)} %select_maximum_fusion.2), kind=kLoop, calls=%fused_computation.4.clone.1 | loop fusion | flops 9434112 | bytes 12607488 | tf_op jit(solution)/shard_map/while/body/eval_jaxpr/reduce_sum | solution.py:26
  456.0 5.4 fusion.38
  461.3 7.8 %bitcast_reduce_fusion.2 = (f32[3,1024]{1,0:T(4,128)S(1)}, f32[3,1024,1024]{2,1,0:T(8,128)}) fusion(bf16[1024,3,128]{2,0,1:T(8,128)(2,1)} %get-tuple-element.182, bf16[16,1024,3,128]{3,1,0,2:T(8,128)(2,1)} %get-tuple-element.181, s32[]{:T(128)} %get-tuple-element.168), kind=kOutput, calls=%fused_computation.1.clone.1 | convolution fusion | flops 811594752 | bytes 14168576 | tf_op jit(solution)/shard_map/while/body/eval_jaxpr/qhd,khd->hqk/dot_general | solution.py:21
  469.1 6.8 %fusion.36 = f32[3,1024]{1,0:T(4,128)S(1)} fusion(f32[3,1024,1024]{2,1,0:T(8,128)} %get-tuple-element.156, f32[3,1024]{1,0:T(4,128)S(1)} %select_maximum_fusion.2), kind=kLoop, calls=%fused_computation.4.clone.1 | loop fusion | flops 9434112 | bytes 12607488 | tf_op jit(solution)/shard_map/while/body/eval_jaxpr/reduce_sum | solution.py:26
  477.2 5.4 fusion.38
  482.6 7.8 %bitcast_reduce_fusion.2 = (f32[3,1024]{1,0:T(4,128)S(1)}, f32[3,1024,1024]{2,1,0:T(8,128)}) fusion(bf16[1024,3,128]{2,0,1:T(8,128)(2,1)} %get-tuple-element.182, bf16[16,1024,3,128]{3,1,0,2:T(8,128)(2,1)} %get-tuple-element.181, s32[]{:T(128)} %get-tuple-element.168), kind=kOutput, calls=%fused_computation.1.clone.1 | convolution fusion | flops 811594752 | bytes 14168576 | tf_op jit(solution)/shard_map/while/body/eval_jaxpr/qhd,khd->hqk/dot_general | solution.py:21
  490.4 6.8 %fusion.36 = f32[3,1024]{1,0:T(4,128)S(1)} fusion(f32[3,1024,1024]{2,1,0:T(8,128)} %get-tuple-element.156, f32[3,1024]{1,0:T(4,128)S(1)} %select_maximum_fusion.2), kind=kLoop, calls=%fused_computation.4.clone.1 | loop fusion | flops 9434112 | bytes 12607488 | tf_op jit(solution)/shard_map/while/body/eval_jaxpr/reduce_sum | solution.py:26
  498.5 5.4 fusion.38
  503.9 7.8 %bitcast_reduce_fusion.2 = (f32[3,1024]{1,0:T(4,128)S(1)}, f32[3,1024,1024]{2,1,0:T(8,128)}) fusion(bf16[1024,3,128]{2,0,1:T(8,128)(2,1)} %get-tuple-element.182, bf16[16,1024,3,128]{3,1,0,2:T(8,128)(2,1)} %get-tuple-element.181, s32[]{:T(128)} %get-tuple-element.168), kind=kOutput, calls=%fused_computation.1.clone.1 | convolution fusion | flops 811594752 | bytes 14168576 | tf_op jit(solution)/shard_map/while/body/eval_jaxpr/qhd,khd->hqk/dot_general | solution.py:21
  511.7 6.8 %fusion.36 = f32[3,1024]{1,0:T(4,128)S(1)} fusion(f32[3,1024,1024]{2,1,0:T(8,128)} %get-tuple-element.156, f32[3,1024]{1,0:T(4,128)S(1)} %select_maximum_fusion.2), kind=kLoop, calls=%fused_computation.4.clone.1 | loop fusion | flops 9434112 | bytes 12607488 | tf_op jit(solution)/shard_map/while/body/eval_jaxpr/reduce_sum | solution.py:26
  519.8 5.4 fusion.38
  525.2 7.8 %bitcast_reduce_fusion.2 = (f32[3,1024]{1,0:T(4,128)S(1)}, f32[3,1024,1024]{2,1,0:T(8,128)}) fusion(bf16[1024,3,128]{2,0,1:T(8,128)(2,1)} %get-tuple-element.182, bf16[16,1024,3,128]{3,1,0,2:T(8,128)(2,1)} %get-tuple-element.181, s32[]{:T(128)} %get-tuple-element.168), kind=kOutput, calls=%fused_computation.1.clone.1 | convolution fusion | flops 811594752 | bytes 14168576 | tf_op jit(solution)/shard_map/while/body/eval_jaxpr/qhd,khd->hqk/dot_general | solution.py:21
  532.9 6.8 %fusion.36 = f32[3,1024]{1,0:T(4,128)S(1)} fusion(f32[3,1024,1024]{2,1,0:T(8,128)} %get-tuple-element.156, f32[3,1024]{1,0:T(4,128)S(1)} %select_maximum_fusion.2), kind=kLoop, calls=%fused_computation.4.clone.1 | loop fusion | flops 9434112 | bytes 12607488 | tf_op jit(solution)/shard_map/while/body/eval_jaxpr/reduce_sum | solution.py:26
  541.1 5.4 fusion.38
  546.5 1.9 fusion.25
  548.9 21.4 %all_to_all.66 = bf16[8,128,384]{1,2,0:T(8,128)(2,1)S(1)} all-to-all(bf16[8,128,384]{1,2,0:T(8,128)(2,1)S(1)} %copy.42), channel_id=1, replica_groups=mesh['blk'=16,'head'=8] {'head'}, dimensions={0} | all-to-all | bytes 1572864 | tf_op jit(solution)/shard_map/all_to_all | solution.py:72
  (108 shorter events, 27.6 us)
Async XLA Ops:
  6.5 107.5 %all-gather.3.cloned.1.call-start = ((), (), s32[]{:S(2)}) async-start(), calls=%async_computation.4 | async-start | bytes 13369344 | tf_op jit(solution)/shard_map/all_gather | solution.py:57
  32.2 1.3 copy-start.2
  33.5 156.2 %all-gather.5.cloned.1.call-start = ((), (), s32[]{:S(2)}) async-start(), calls=%async_computation.5 | async-start | bytes 13369344 | tf_op jit(solution)/shard_map/all_gather | solution.py:58
  55.4 1.3 copy-start.1
  55.4 1.5 copy-start.3
  58.4 22.4 %all-to-all-start.1 = ((bf16[128,8,384]{0,2,1:T(8,128)(2,1)}), bf16[128,8,384]{0,2,1:T(8,128)(2,1)S(1)}, u32[]{:S(2)}, u32[]{:S(2)}) async-start(bf16[128,8,384]{0,2,1:T(8,128)(2,1)} %bitcast.3), calls=%async_computation.1 | async-start | bytes 1572864 | tf_op jit(solution)/shard_map/all_to_all | solution.py:44
  214.0 8.2 %copy-start = (f32[3,1024,1024]{2,1,0:T(8,128)S(1)}, f32[3,1024,1024]{2,1,0:T(8,128)}, u32[]{:S(2)}) copy-start(f32[3,1024,1024]{2,1,0:T(8,128)} %get-tuple-element.156) | copy-start | bytes 37748740 | tf_op jit(solution)/shard_map/while
  235.0 8.2 %copy-start = (f32[3,1024,1024]{2,1,0:T(8,128)S(1)}, f32[3,1024,1024]{2,1,0:T(8,128)}, u32[]{:S(2)}) copy-start(f32[3,1024,1024]{2,1,0:T(8,128)} %get-tuple-element.156) | copy-start | bytes 37748740 | tf_op jit(solution)/shard_map/while
  256.3 8.2 %copy-start = (f32[3,1024,1024]{2,1,0:T(8,128)S(1)}, f32[3,1024,1024]{2,1,0:T(8,128)}, u32[]{:S(2)}) copy-start(f32[3,1024,1024]{2,1,0:T(8,128)} %get-tuple-element.156) | copy-start | bytes 37748740 | tf_op jit(solution)/shard_map/while
  277.6 8.2 %copy-start = (f32[3,1024,1024]{2,1,0:T(8,128)S(1)}, f32[3,1024,1024]{2,1,0:T(8,128)}, u32[]{:S(2)}) copy-start(f32[3,1024,1024]{2,1,0:T(8,128)} %get-tuple-element.156) | copy-start | bytes 37748740 | tf_op jit(solution)/shard_map/while
  298.9 8.2 %copy-start = (f32[3,1024,1024]{2,1,0:T(8,128)S(1)}, f32[3,1024,1024]{2,1,0:T(8,128)}, u32[]{:S(2)}) copy-start(f32[3,1024,1024]{2,1,0:T(8,128)} %get-tuple-element.156) | copy-start | bytes 37748740 | tf_op jit(solution)/shard_map/while
  320.1 8.2 %copy-start = (f32[3,1024,1024]{2,1,0:T(8,128)S(1)}, f32[3,1024,1024]{2,1,0:T(8,128)}, u32[]{:S(2)}) copy-start(f32[3,1024,1024]{2,1,0:T(8,128)} %get-tuple-element.156) | copy-start | bytes 37748740 | tf_op jit(solution)/shard_map/while
  341.4 8.2 %copy-start = (f32[3,1024,1024]{2,1,0:T(8,128)S(1)}, f32[3,1024,1024]{2,1,0:T(8,128)}, u32[]{:S(2)}) copy-start(f32[3,1024,1024]{2,1,0:T(8,128)} %get-tuple-element.156) | copy-start | bytes 37748740 | tf_op jit(solution)/shard_map/while
  362.7 8.2 %copy-start = (f32[3,1024,1024]{2,1,0:T(8,128)S(1)}, f32[3,1024,1024]{2,1,0:T(8,128)}, u32[]{:S(2)}) copy-start(f32[3,1024,1024]{2,1,0:T(8,128)} %get-tuple-element.156) | copy-start | bytes 37748740 | tf_op jit(solution)/shard_map/while
  384.0 8.2 %copy-start = (f32[3,1024,1024]{2,1,0:T(8,128)S(1)}, f32[3,1024,1024]{2,1,0:T(8,128)}, u32[]{:S(2)}) copy-start(f32[3,1024,1024]{2,1,0:T(8,128)} %get-tuple-element.156) | copy-start | bytes 37748740 | tf_op jit(solution)/shard_map/while
  405.3 8.2 %copy-start = (f32[3,1024,1024]{2,1,0:T(8,128)S(1)}, f32[3,1024,1024]{2,1,0:T(8,128)}, u32[]{:S(2)}) copy-start(f32[3,1024,1024]{2,1,0:T(8,128)} %get-tuple-element.156) | copy-start | bytes 37748740 | tf_op jit(solution)/shard_map/while
  426.5 8.2 %copy-start = (f32[3,1024,1024]{2,1,0:T(8,128)S(1)}, f32[3,1024,1024]{2,1,0:T(8,128)}, u32[]{:S(2)}) copy-start(f32[3,1024,1024]{2,1,0:T(8,128)} %get-tuple-element.156) | copy-start | bytes 37748740 | tf_op jit(solution)/shard_map/while
  447.8 8.2 %copy-start = (f32[3,1024,1024]{2,1,0:T(8,128)S(1)}, f32[3,1024,1024]{2,1,0:T(8,128)}, u32[]{:S(2)}) copy-start(f32[3,1024,1024]{2,1,0:T(8,128)} %get-tuple-element.156) | copy-start | bytes 37748740 | tf_op jit(solution)/shard_map/while
  469.1 8.2 %copy-start = (f32[3,1024,1024]{2,1,0:T(8,128)S(1)}, f32[3,1024,1024]{2,1,0:T(8,128)}, u32[]{:S(2)}) copy-start(f32[3,1024,1024]{2,1,0:T(8,128)} %get-tuple-element.156) | copy-start | bytes 37748740 | tf_op jit(solution)/shard_map/while
  490.4 8.2 %copy-start = (f32[3,1024,1024]{2,1,0:T(8,128)S(1)}, f32[3,1024,1024]{2,1,0:T(8,128)}, u32[]{:S(2)}) copy-start(f32[3,1024,1024]{2,1,0:T(8,128)} %get-tuple-element.156) | copy-start | bytes 37748740 | tf_op jit(solution)/shard_map/while
  511.7 8.2 %copy-start = (f32[3,1024,1024]{2,1,0:T(8,128)S(1)}, f32[3,1024,1024]{2,1,0:T(8,128)}, u32[]{:S(2)}) copy-start(f32[3,1024,1024]{2,1,0:T(8,128)} %get-tuple-element.156) | copy-start | bytes 37748740 | tf_op jit(solution)/shard_map/while
  532.9 8.2 %copy-start = (f32[3,1024,1024]{2,1,0:T(8,128)S(1)}, f32[3,1024,1024]{2,1,0:T(8,128)}, u32[]{:S(2)}) copy-start(f32[3,1024,1024]{2,1,0:T(8,128)} %get-tuple-element.156) | copy-start | bytes 37748740 | tf_op jit(solution)/shard_map/while
Sparse Core Ops, SparseCore 0:
  33.6 80.3 all-gather.2
  115.7 73.9 all-gather.4
where the time goes:
time: 580 us; the launch traced here: 578 us
  matrix products  209 us (36%)
  other arithmetic  114 us (20%)
  waiting for transfers between devices  109 us (19%)
  blocking collectives  64.4 us (11%)
  local copies, waits for them, and re-layouts  63.7 us (11%)
  between operations  13.6 us (2%)
    dot_general x16, matrix products, absorb(): jnp.einsum('qhd,khd->hqk', q_heads, key_block, preferred_element_type=jnp...  124 us
    reduce_sum x16, other arithmetic, absorb(): new_sum = run_sum * shrink + jnp.sum(weights, axis=-1)  109 us
    dot_general x16, matrix products, absorb(): jnp.einsum('hqk,khd->hqd', weights.astype(jnp.bfloat16), value_block, pre...  85.5 us
    all_gather x1, waiting for transfers between devices, shards(): value_piece = lax.all_gather(v_heads, 'blk', axis=0, tiled=True)  59 us
    all_gather x1, waiting for transfers between devices, shards(): key_piece = lax.all_gather(k_heads, 'blk', axis=0, tiled=True)  31.2 us
    all_to_all x1, blocking collectives, shards(): lax.all_to_all(second_part, 'head', split_axis=1, concat_axis=0, tiled=True)  22 us
    all_to_all x1, blocking collectives, shards(): lax.all_to_all(result, 'head', split_axis=0, concat_axis=1, tiled=True)  21.4 us
    while x48, local copies, waits for them, and re-layouts  21.4 us
  transfers between devices with their start and end apart: 3, of which 3 were waited for; matrix products, arithmetic and copies ran while one was open for 4% of the time, Pallas kernels for 0%

commit v1 on v0

v1 whole, which is shorter than its diff:
```python
import functools
import math

import jax
import jax.numpy as jnp
from jax import lax
from jax.experimental import pallas as pl
from jax.experimental.pallas import tpu as pltpu
from jax.sharding import PartitionSpec as P

HEAD_DIM = 128
EPS = 1e-06
HPG = 3
GROUPS = 8
TOK = 128
ROWS = TOK * GROUPS
BQ = 512
KEYS = 2 * ROWS
SCALE = math.log2(math.e) / math.sqrt(HEAD_DIM)
MESH = pl.DeviceIdType.MESH
PAIRS = 24
FORWARD_NEAR = {3: 0, 5: 1, 8: 2}
FORWARD_FAR = {9: 0, 11: 1, 14: 2}


def place(p):
    last = p >= 18
    chunk = p // 6
    head = jnp.where(last, (p - 18) % 3, (p % 6) // 2)
    half = jnp.where(last, 1 - (p - 18) // 3, p % 2)
    return chunk, head, half


def normed(wide, gain):
    mean_sq = jnp.mean(wide * wide, axis=-1, keepdims=True)
    return (wide * lax.rsqrt(mean_sq + EPS) * gain).astype(jnp.bfloat16)


def kernel(
    q_in, k_in, v_in, qg_ref, kg_ref, o_ref,
    qn, kn, k_all, v_all, q_all, scores, shrink, top, acc,
    part_out, part_in, lse_out, lse_in, o_out, o_in,
    kv_recv, kv_send, q_recv, q_send, in_send, part_sem, o_send, o_recv,
):
    b = lax.axis_index("blk")
    c = lax.axis_index("head")
    side = b // 8
    y = (b // 2) % 4
    core = b % 2
    other_core = (b + 1 - 2 * core, c)
    above = (side * 8 + ((y + 1) % 4) * 2 + core, c)
    below = (side * 8 + ((y + 3) % 4) * 2 + core, c)
    across = ((b + 8) % 16, c)

    def remote(src, dst, send, recv, dev):
        return pltpu.make_async_remote_copy(
            src_ref=src, dst_ref=dst, send_sem=send, recv_sem=recv,
            device_id=dev, device_id_type=MESH,
        )

    def await_bytes(ref, sem):
        pltpu.make_async_copy(ref, ref, sem).wait()

    def cols(n):
        return pl.ds(pl.multiple_of(n * HEAD_DIM, HEAD_DIM), HEAD_DIM)

    def rows_of(g):
        return pl.ds(pl.multiple_of(g * TOK, TOK), TOK)

    def k_chunk(h, slot, core_slot):
        return k_all.at[h, slot, pl.ds(core_slot * ROWS, ROWS), :]

    def v_chunk(h, slot, core_slot):
        return v_all.at[h, slot, pl.ds(core_slot * ROWS, ROWS), pl.ds(0, HEAD_DIM)]

    v_all[:, :, :, HEAD_DIM:] = jnp.ones((HPG, 4, KEYS, HEAD_DIM), jnp.bfloat16)

    barrier = pltpu.get_barrier_semaphore()
    partners = [(b, (c + d) % GROUPS) for d in range(1, GROUPS)]
    partners += [other_core, above, below, across]
    for dev in partners:
        pl.semaphore_signal(barrier, inc=1, device_id=dev, device_id_type=MESH)
    kn[...] = normed(k_in[...].astype(jnp.float32), kg_ref[...])
    pl.semaphore_wait(barrier, len(partners))

    def scatter(src, dst_of, kind, recv, h):
        mine = pltpu.make_async_copy(
            src.at[:, cols(c * HPG + h)], dst_of(rows_of(c)), recv
        )
        mine.start()
        for d in range(1, GROUPS):
            g = (c + d) % GROUPS
            remote(
                src.at[:, cols(g * HPG + h)], dst_of(rows_of(c)),
                in_send.at[kind, h], recv, (b, g),
            ).start()

    def scatter_k(h):
        scatter(kn, lambda r: k_all.at[h, 0, r, :], 0, kv_recv.at[0, h, 0, 0], h)

    def scatter_v(h):
        scatter(
            v_in, lambda r: v_all.at[h, 0, r, pl.ds(0, HEAD_DIM)], 1,
            kv_recv.at[1, h, 0, 0], h,
        )

    def scatter_q(h):
        scatter(qn, lambda r: q_all.at[h, 0, r, :], 2, q_recv.at[h, 0], h)

    scatter_k(0)
    scatter_v(0)
    qn[...] = normed(q_in[...].astype(jnp.float32), qg_ref[...])
    scatter_q(0)
    for h in range(1, HPG):
        scatter_k(h)
        scatter_v(h)
        scatter_q(h)
    acc[...] = jnp.zeros_like(acc)
    top[...] = jnp.full_like(top, -1e30)

    def send_own(h):
        await_bytes(k_chunk(h, 0, 0), kv_recv.at[0, h, 0, 0])
        await_bytes(v_chunk(h, 0, 0), kv_recv.at[1, h, 0, 0])
        for t, chunk in ((0, k_chunk), (1, v_chunk)):
            mine = chunk(h, 0, 0)
            remote(mine, chunk(h, 0, 1), kv_send.at[t, h, 0, 0],
                   kv_recv.at[t, h, 0, 1], other_core).start()
            remote(mine, chunk(h, 1, 0), kv_send.at[t, h, 0, 1],
                   kv_recv.at[t, h, 1, 0], above).start()
            remote(mine, chunk(h, 2, 0), kv_send.at[t, h, 0, 2],
                   kv_recv.at[t, h, 2, 0], below).start()
        await_bytes(q_all.at[h, 0], q_recv.at[h, 0])
        remote(q_all.at[h, 0], q_all.at[h, 1], q_send.at[h],
               q_recv.at[h, 1], across).start()

    def to_other_core(t, h, slot):
        chunk = (k_chunk, v_chunk)[t]
        remote(chunk(h, slot, 0), chunk(h, slot, 1), kv_send.at[t, h, slot, 0],
               kv_recv.at[t, h, slot, 1], other_core).start()

    def forward_near(h):
        for t, chunk in ((0, k_chunk), (1, v_chunk)):
            for slot in (1, 2):
                await_bytes(chunk(h, slot, 0), kv_recv.at[t, h, slot, 0])
        remote(k_chunk(h, 1, 0), k_chunk(h, 3, 0), kv_send.at[0, h, 1, 1],
               kv_recv.at[0, h, 3, 0], above).start()
        remote(v_chunk(h, 2, 0), v_chunk(h, 3, 0), kv_send.at[1, h, 2, 1],
               kv_recv.at[1, h, 3, 0], below).start()
        for slot in (1, 2):
            for t in (0, 1):
                to_other_core(t, h, slot)

    def forward_far(h):
        for t, chunk in ((0, k_chunk), (1, v_chunk)):
            await_bytes(chunk(h, 3, 0), kv_recv.at[t, h, 3, 0])
            to_other_core(t, h, 3)

    def score_step(p, block, slot):
        chunk, h, half = place(p)
        rows = pl.ds(block * BQ, BQ)
        s = lax.dot_general(
            q_all[h, half, rows, :], k_all[h, chunk], (((1,), (1,)), ((), ())),
            preferred_element_type=jnp.float32,
        )
        scores[slot] = s
        old = top[h, half, rows, :]
        new = jnp.maximum(old, jnp.max(s, axis=1, keepdims=True))
        top[h, half, rows, :] = new
        shrink[slot] = jnp.exp2((old - new) * SCALE)

    def value_step(p, block, slot):
        chunk, h, half = place(p)
        rows = pl.ds(block * BQ, BQ)
        weights = jnp.exp2(scores[slot] * SCALE - top[h, half, rows, :] * SCALE)
        mixed = jnp.dot(
            weights.astype(jnp.bfloat16), v_all[h, chunk],
            preferred_element_type=jnp.float32,
        )
        acc[h, half, rows, :] = acc[h, half, rows, :] * shrink[slot] + mixed

    def before(p):
        chunk, h, half = place(p)

        @pl.when(jnp.logical_and(p < 6, p % 2 == 0))
        def _():
            await_bytes(k_chunk(h, 0, 1), kv_recv.at[0, h, 0, 1])
            await_bytes(v_chunk(h, 0, 1), kv_recv.at[1, h, 0, 1])

        @pl.when(jnp.logical_and(p < 6, p % 2 == 1))
        def _():
            await_bytes(q_all.at[h, 1], q_recv.at[h, 1])

        late = jnp.logical_and(p >= 6, p < 18)

        @pl.when(jnp.logical_or(jnp.logical_and(late, p % 2 == 0),
                                jnp.logical_and(p >= 18, p < 21)))
        def _():
            await_bytes(k_chunk(h, chunk, 1), kv_recv.at[0, h, chunk, 1])
            await_bytes(v_chunk(h, chunk, 1), kv_recv.at[1, h, chunk, 1])

    def finish_block(h, half, block):
        rows = pl.ds(block * BQ, BQ)
        total = acc[h, half, rows, HEAD_DIM:]
        mean = acc[h, half, rows, :HEAD_DIM] / total
        lse = top[h, half, rows, :] * SCALE + jnp.log2(total)
        return mean, lse

    def send_part(h):
        for block in range(ROWS // BQ):
            rows = pl.ds(block * BQ, BQ)
            mean, lse = finish_block(h, 1, block)
            part_out[h, rows, :] = mean.astype(jnp.bfloat16)
            lse_out[h, :, rows] = jnp.transpose(lse)[:8]
        remote(part_out.at[h], part_in.at[h], part_sem.at[0, h, 0],
               part_sem.at[1, h, 0], across).start()
        remote(lse_out.at[h], lse_in.at[h], part_sem.at[0, h, 1],
               part_sem.at[1, h, 1], across).start()

    def send_result(h):
        await_bytes(part_in.at[h], part_sem.at[1, h, 0])
        await_bytes(lse_in.at[h], part_sem.at[1, h, 1])
        for block in range(ROWS // BQ):
            rows = pl.ds(block * BQ, BQ)
            mean, lse = finish_block(h, 0, block)
            row = jnp.broadcast_to(lse_in[h, 0:1, rows], (HEAD_DIM, BQ))
            lse2 = jnp.transpose(row)
            peak = jnp.maximum(lse, lse2)
            w1 = jnp.exp2(lse - peak)
            w2 = jnp.exp2(lse2 - peak)
            both = mean * w1 + part_in[h, rows, :].astype(jnp.float32) * w2
            o_out[h, rows, :] = (both / (w1 + w2)).astype(jnp.bfloat16)
        target = cols(c * HPG + h)
        pltpu.make_async_copy(
            o_out.at[h, rows_of(c), :], o_in.at[:, target], o_recv.at[h]
        ).start()
        for d in range(1, GROUPS):
            g = (c + d) % GROUPS
            remote(o_out.at[h, rows_of(g), :], o_in.at[:, target],
                   o_send.at[h], o_recv.at[h], (b, g)).start()

    send_own(0)
    before(0)
    score_step(0, 0, 0)

    def pair(p, carry):
        score_step(p, 1, 1)
        value_step(p, 0, 0)

        for h in range(1, HPG):
            @pl.when(p == 2 * h - 1)
            def _():
                send_own(h)
        for at, h in FORWARD_NEAR.items():
            @pl.when(p == at)
            def _():
                forward_near(h)
        for at, h in FORWARD_FAR.items():
            @pl.when(p == at)
            def _():
                forward_far(h)

        nxt = jnp.minimum(p + 1, PAIRS - 1)

        @pl.when(p < PAIRS - 1)
        def _():
            before(nxt)

        score_step_next(p)
        value_step(p, 1, 1)

        for h in range(HPG):
            @pl.when(p == 18 + h)
            def _():
                send_part(h)

            @pl.when(p == 21 + h)
            def _():
                send_result(h)
        return carry

    def score_step_next(p):
        score_step(p + 1, 0, 0)

    lax.fori_loop(0, PAIRS - 1, pair, 0)
    p = PAIRS - 1
    score_step(p, 1, 1)
    value_step(p, 0, 0)
    value_step(p, 1, 1)
    send_result(HPG - 1)

    for h in range(HPG):
        await_bytes(o_out.at[h], o_recv.at[h])
    o_ref[...] = o_in[...]

    seven = pl.ds(0, (GROUPS - 1) * TOK)
    for h in range(HPG):
        await_bytes(o_out.at[h, seven, :], o_send.at[h])
        await_bytes(part_out.at[h], part_sem.at[0, h, 0])
        await_bytes(lse_out.at[h], part_sem.at[0, h, 1])
        await_bytes(q_all.at[h, 0], q_send.at[h])
        for kind in range(3):
            await_bytes(o_out.at[h, seven, :], in_send.at[kind, h])
        for t, chunk in ((0, k_chunk), (1, v_chunk)):
            for i in range(3):
                await_bytes(chunk(h, 0, 0), kv_send.at[t, h, 0, i])
            for slot in (1, 2, 3):
                await_bytes(chunk(h, slot, 0), kv_send.at[t, h, slot, 0])
        await_bytes(k_chunk(h, 1, 0), kv_send.at[0, h, 1, 1])
        await_bytes(v_chunk(h, 2, 0), kv_send.at[1, h, 2, 1])


def shards(queries, keys, values, query_gain, key_gain):
    bf16, f32 = jnp.bfloat16, jnp.float32
    dma = pltpu.SemaphoreType.DMA
    width = queries.shape[1]
    halves = (HPG, 2, ROWS)
    return pl.pallas_call(
        kernel,
        out_shape=jax.ShapeDtypeStruct((TOK, width), bf16),
        in_specs=[pl.BlockSpec(memory_space=pltpu.VMEM)] * 5,
        out_specs=pl.BlockSpec(memory_space=pltpu.VMEM),
        scratch_shapes=[
            pltpu.VMEM((TOK, width), bf16),
            pltpu.VMEM((TOK, width), bf16),
            pltpu.VMEM((HPG, 4, KEYS, HEAD_DIM), bf16),
            pltpu.VMEM((HPG, 4, KEYS, 2 * HEAD_DIM), bf16),
            pltpu.VMEM((*halves, HEAD_DIM), bf16),
            pltpu.VMEM((2, BQ, KEYS), f32),
            pltpu.VMEM((2, BQ, 1), f32),
            pltpu.VMEM((*halves, 1), f32),
            pltpu.VMEM((*halves, 2 * HEAD_DIM), f32),
            pltpu.VMEM((HPG, ROWS, HEAD_DIM), bf16),
            pltpu.VMEM((HPG, ROWS, HEAD_DIM), bf16),
            pltpu.VMEM((HPG, 8, ROWS), f32),
            pltpu.VMEM((HPG, 8, ROWS), f32),
            pltpu.VMEM((HPG, ROWS, HEAD_DIM), bf16),
            pltpu.VMEM((TOK, width), bf16),
            dma((2, HPG, 4, 2)),
            dma((2, HPG, 4, 3)),
            dma((HPG, 2)),
            dma((HPG,)),
            dma((3, HPG)),
            dma((2, HPG, 2)),
            dma((HPG,)),
            dma((HPG,)),
        ],
        compiler_params=pltpu.CompilerParams(
            collective_id=0, has_side_effects=True, vmem_limit_bytes=60 << 20
        ),
    )(queries, keys, values, query_gain.reshape(1, width), key_gain.reshape(1, width))


def solution(mesh):
    rows = P(("blk", "head"), None)
    return jax.shard_map(
        shards, mesh=mesh, in_specs=(rows, rows, rows, P(), P()), out_specs=rows,
        check_vma=False,
    )
```

time: 580 us -> 159 us (0.27)
  matrix products: 209 us -> 0 us
  Pallas kernels: 0 us -> 157 us
  other arithmetic: 114 us -> 0 us
  waiting for transfers between devices: 109 us -> 0 us
  blocking collectives: 64.4 us -> 0 us
  local copies, waits for them, and re-layouts: 63.7 us -> 2.06 us
  between operations: 13.6 us -> 0.01 us
    dot_general x32 -> x0, matrix products: 209 us -> none  [the longest x16 124 us: absorb(): jnp.einsum('qhd,khd->hqk', q_heads, key_block, preferred_element_type=jnp...]
    pallas_call x0 -> x1, Pallas kernels: none -> 157 us  [shards(): pl.pallas_call(kernel, out_shape=jax.ShapeDtypeStruct((TOK, width), bf16)...]
    reduce_sum x18 -> x0, other arithmetic: 110 us -> none  [the longest x16 109 us: absorb(): new_sum = run_sum * shrink + jnp.sum(weights, axis=-1)]
    all_gather x2 -> x0, waiting for transfers between devices: 90.1 us -> none  [the longest x1 59 us: shards(): value_piece = lax.all_gather(v_heads, 'blk', axis=0, tiled=True)]
    all_to_all x3 -> x0, blocking collectives: 64.4 us -> none  [the longest x1 22 us: shards(): lax.all_to_all(second_part, 'head', split_axis=1, concat_axis=0, tiled=True)]
    all_gather x2 -> x0, local copies, waits for them, and re-layouts: 33.2 us -> none  [the longest x1 16.7 us: shards(): key_piece = lax.all_gather(k_heads, 'blk', axis=0, tiled=True)]
    while x48 -> x0, local copies, waits for them, and re-layouts: 21.4 us -> none
    all_to_all x1 -> x0, waiting for transfers between devices: 18.7 us -> none  [shards(): lax.all_to_all(first_part, 'head', split_axis=1, concat_axis=0, tiled=True)]
  transfers between devices with their start and end apart: 3 -> 0, of which waited for: 3 -> 0; matrix products, arithmetic and copies ran while one was open for 4% -> 0% of each run, Pallas kernels for 0% -> 0%
where the time goes in v1:
time: 159 us
  Pallas kernels  157 us (99%)
  local copies, waits for them, and re-layouts  2.06 us (1%)
    pallas_call x1, Pallas kernels, shards(): pl.pallas_call(kernel, out_shape=jax.ShapeDtypeStruct((TOK, width), bf16)...  157 us

profile of v1, /device:TPU:0, one launch (start us, length us, event | category | flops | bytes accessed | tf_op | source)
XLA Modules:
  0.0 158.9 jit_solution(4912912593725506743)
XLA Ops:
  0.0 156.8 %shard_map.55 = bf16[128,3072]{1,0:T(8,128)(2,1)} custom-call(bf16[128,3072]{1,0:T(8,128)(2,1)} %q_in.1, bf16[128,3072]{1,0:T(8,128)(2,1)} %k_in.1, bf16[128,3072]{1,0:T(8,128)(2,1)} %v_in.1, f32[1,3072]{1,0:T(1,128)} %bitcast.2, f32[1,3072]{1,0:T(1,128)} %bitcast.3), custom_call_target="tpu_custom_call" | custom-call | tf_op jit(solution)/shard_map/pallas_call | solution.py:317
  156.8 2.1 %copy.7 = bf16[128,3072]{1,0:T(8,128)(2,1)} copy(bf16[128,3072]{1,0:T(8,128)(2,1)} %shard_map.55) | data formatting | bytes 1572864

commit v2 on v1

--- a/solution.py
+++ b/solution.py
@@ -38,7 +38,7 @@
 
 def kernel(
     q_in, k_in, v_in, qg_ref, kg_ref, o_ref,
-    qn, kn, k_all, v_all, q_all, scores, shrink, top, acc,
+    qn, kn, k_all, v_all, q_all, scores, shrink, peak, top, acc,
     part_out, part_in, lse_out, lse_in, o_out, o_in,
     kv_recv, kv_send, q_recv, q_send, in_send, part_sem, o_send, o_recv,
 ):
@@ -111,10 +111,6 @@
     scatter_v(0)
     qn[...] = normed(q_in[...].astype(jnp.float32), qg_ref[...])
     scatter_q(0)
-    for h in range(1, HPG):
-        scatter_k(h)
-        scatter_v(h)
-        scatter_q(h)
     acc[...] = jnp.zeros_like(acc)
     top[...] = jnp.full_like(top, -1e30)
 
@@ -166,12 +162,13 @@
         old = top[h, half, rows, :]
         new = jnp.maximum(old, jnp.max(s, axis=1, keepdims=True))
         top[h, half, rows, :] = new
+        peak[slot] = new * SCALE
         shrink[slot] = jnp.exp2((old - new) * SCALE)
 
     def value_step(p, block, slot):
         chunk, h, half = place(p)
         rows = pl.ds(block * BQ, BQ)
-        weights = jnp.exp2(scores[slot] * SCALE - top[h, half, rows, :] * SCALE)
+        weights = jnp.exp2(scores[slot] * SCALE - peak[slot])
         mixed = jnp.dot(
             weights.astype(jnp.bfloat16), v_all[h, chunk],
             preferred_element_type=jnp.float32,
@@ -224,9 +221,9 @@
             mean, lse = finish_block(h, 0, block)
             row = jnp.broadcast_to(lse_in[h, 0:1, rows], (HEAD_DIM, BQ))
             lse2 = jnp.transpose(row)
-            peak = jnp.maximum(lse, lse2)
-            w1 = jnp.exp2(lse - peak)
-            w2 = jnp.exp2(lse2 - peak)
+            high = jnp.maximum(lse, lse2)
+            w1 = jnp.exp2(lse - high)
+            w2 = jnp.exp2(lse2 - high)
             both = mean * w1 + part_in[h, rows, :].astype(jnp.float32) * w2
             o_out[h, rows, :] = (both / (w1 + w2)).astype(jnp.bfloat16)
         target = cols(c * HPG + h)
@@ -238,7 +235,21 @@
             remote(o_out.at[h, rows_of(g), :], o_in.at[:, target],
                    o_send.at[h], o_recv.at[h], (b, g)).start()
 
+    seven = pl.ds(0, (GROUPS - 1) * TOK)
+
+    def scatter_done(h):
+        for kind in range(3):
+            await_bytes(o_out.at[h, seven, :], in_send.at[kind, h])
+
+    scatter_done(0)
+    scatter_k(1)
+    scatter_v(1)
+    scatter_q(1)
     send_own(0)
+    scatter_done(1)
+    scatter_k(2)
+    scatter_v(2)
+    scatter_q(2)
     before(0)
     score_step(0, 0, 0)
 
@@ -292,14 +303,12 @@
         await_bytes(o_out.at[h], o_recv.at[h])
     o_ref[...] = o_in[...]
 
-    seven = pl.ds(0, (GROUPS - 1) * TOK)
+    scatter_done(2)
     for h in range(HPG):
         await_bytes(o_out.at[h, seven, :], o_send.at[h])
         await_bytes(part_out.at[h], part_sem.at[0, h, 0])
         await_bytes(lse_out.at[h], part_sem.at[0, h, 1])
         await_bytes(q_all.at[h, 0], q_send.at[h])
-        for kind in range(3):
-            await_bytes(o_out.at[h, seven, :], in_send.at[kind, h])
         for t, chunk in ((0, k_chunk), (1, v_chunk)):
             for i in range(3):
                 await_bytes(chunk(h, 0, 0), kv_send.at[t, h, 0, i])
@@ -326,6 +335,7 @@
             pltpu.VMEM((HPG, 4, KEYS, 2 * HEAD_DIM), bf16),
             pltpu.VMEM((*halves, HEAD_DIM), bf16),
             pltpu.VMEM((2, BQ, KEYS), f32),
+            pltpu.VMEM((2, BQ, 1), f32),
             pltpu.VMEM((2, BQ, 1), f32),
             pltpu.VMEM((*halves, 1), f32),
             pltpu.VMEM((*halves, 2 * HEAD_DIM), f32),

time: 159 us -> 133 us (0.84)
  Pallas kernels: 157 us -> 131 us
    pallas_call x1, Pallas kernels: 157 us -> 131 us  [shards(): pl.pallas_call(kernel, out_shape=jax.ShapeDtypeStruct((TOK, width), bf16)...]
where the time goes in v2:
time: 133 us
  Pallas kernels  131 us (98%)
  local copies, waits for them, and re-layouts  2.06 us (2%)
    pallas_call x1, Pallas kernels, shards(): pl.pallas_call(kernel, out_shape=jax.ShapeDtypeStruct((TOK, width), bf16)...  131 us

profile of v2, /device:TPU:0, one launch (start us, length us, event | category | flops | bytes accessed | tf_op | source)
XLA Modules:
  0.0 133.1 jit_solution(10829287789124344047)
XLA Ops:
  0.0 131.1 %shard_map.55 = bf16[128,3072]{1,0:T(8,128)(2,1)} custom-call(bf16[128,3072]{1,0:T(8,128)(2,1)} %q_in.1, bf16[128,3072]{1,0:T(8,128)(2,1)} %k_in.1, bf16[128,3072]{1,0:T(8,128)(2,1)} %v_in.1, f32[1,3072]{1,0:T(1,128)} %bitcast.2, f32[1,3072]{1,0:T(1,128)} %bitcast.3), custom_call_target="tpu_custom_call" | custom-call | tf_op jit(solution)/shard_map/pallas_call | solution.py:326
  131.1 2.1 %copy.7 = bf16[128,3072]{1,0:T(8,128)(2,1)} copy(bf16[128,3072]{1,0:T(8,128)(2,1)} %shard_map.55) | data formatting | bytes 1572864

commit v3 on v2

--- a/solution.py
+++ b/solution.py
@@ -18,17 +18,42 @@
 KEYS = 2 * ROWS
 SCALE = math.log2(math.e) / math.sqrt(HEAD_DIM)
 MESH = pl.DeviceIdType.MESH
-PAIRS = 24
-FORWARD_NEAR = {3: 0, 5: 1, 8: 2}
-FORWARD_FAR = {9: 0, 11: 1, 14: 2}
+ORDER = (
+    (0, 0, 0), (0, 0, 1), (1, 0, 0), (0, 1, 0), (0, 1, 1), (0, 2, 0),
+    (0, 2, 1), (1, 0, 1), (2, 0, 0), (1, 1, 0), (1, 1, 1), (1, 2, 0),
+    (1, 2, 1), (0, 3, 1), (2, 0, 1), (1, 3, 1), (2, 1, 0), (2, 1, 1),
+    (2, 2, 0), (2, 2, 1), (2, 3, 1), (0, 3, 0), (1, 3, 0), (2, 3, 0),
+)
+PAIRS = len(ORDER)
+FORWARD_NEAR = {7: 1, 11: 2}
+FORWARD_FAR = {8: 0, 12: 1, 17: 2}
+
+
+def first_uses(key):
+    seen, firsts = set(), []
+    for p, entry in enumerate(ORDER):
+        if key(entry) is not None and key(entry) not in seen:
+            seen.add(key(entry))
+            firsts.append(p)
+    return firsts
+
+
+CHUNK_FIRST = first_uses(lambda e: e[:2])
+ACROSS_FIRST = first_uses(lambda e: e[0] if e[2] else None)
+
+
+def one_of(u, options):
+    return functools.reduce(jnp.logical_or, [u == o for o in options])
 
 
 def place(p):
-    last = p >= 18
-    chunk = p // 6
-    head = jnp.where(last, (p - 18) % 3, (p % 6) // 2)
-    half = jnp.where(last, 1 - (p - 18) // 3, p % 2)
-    return chunk, head, half
+    def column(i):
+        value = 0
+        for v in sorted({e[i] for e in ORDER} - {0}):
+            value = jnp.where(one_of(p, [n for n, e in enumerate(ORDER) if e[i] == v]), v, value)
+        return value
+
+    return column(1), column(0), column(2)
 
 
 def normed(wide, gain):
@@ -81,6 +106,7 @@
     for dev in partners:
         pl.semaphore_signal(barrier, inc=1, device_id=dev, device_id_type=MESH)
     kn[...] = normed(k_in[...].astype(jnp.float32), kg_ref[...])
+    qn[...] = normed(q_in[...].astype(jnp.float32), qg_ref[...])
     pl.semaphore_wait(barrier, len(partners))
 
     def scatter(src, dst_of, kind, recv, h):
@@ -107,10 +133,9 @@
     def scatter_q(h):
         scatter(qn, lambda r: q_all.at[h, 0, r, :], 2, q_recv.at[h, 0], h)
 
+    scatter_q(0)
     scatter_k(0)
     scatter_v(0)
-    qn[...] = normed(q_in[...].astype(jnp.float32), qg_ref[...])
-    scatter_q(0)
     acc[...] = jnp.zeros_like(acc)
     top[...] = jnp.full_like(top, -1e30)
 
@@ -125,6 +150,8 @@
                    kv_recv.at[t, h, 1, 0], above).start()
             remote(mine, chunk(h, 2, 0), kv_send.at[t, h, 0, 2],
                    kv_recv.at[t, h, 2, 0], below).start()
+
+    def send_across(h):
         await_bytes(q_all.at[h, 0], q_recv.at[h, 0])
         remote(q_all.at[h, 0], q_all.at[h, 1], q_send.at[h],
                q_recv.at[h, 1], across).start()
@@ -178,22 +205,14 @@
     def before(p):
         chunk, h, half = place(p)
 
-        @pl.when(jnp.logical_and(p < 6, p % 2 == 0))
-        def _():
-            await_bytes(k_chunk(h, 0, 1), kv_recv.at[0, h, 0, 1])
-            await_bytes(v_chunk(h, 0, 1), kv_recv.at[1, h, 0, 1])
-
-        @pl.when(jnp.logical_and(p < 6, p % 2 == 1))
-        def _():
-            await_bytes(q_all.at[h, 1], q_recv.at[h, 1])
-
-        late = jnp.logical_and(p >= 6, p < 18)
-
-        @pl.when(jnp.logical_or(jnp.logical_and(late, p % 2 == 0),
-                                jnp.logical_and(p >= 18, p < 21)))
+        @pl.when(one_of(p, CHUNK_FIRST))
         def _():
             await_bytes(k_chunk(h, chunk, 1), kv_recv.at[0, h, chunk, 1])
             await_bytes(v_chunk(h, chunk, 1), kv_recv.at[1, h, chunk, 1])
+
+        @pl.when(one_of(p, ACROSS_FIRST))
+        def _():
+            await_bytes(q_all.at[h, 1], q_recv.at[h, 1])
 
     def finish_block(h, half, block):
         rows = pl.ds(block * BQ, BQ)
@@ -237,19 +256,16 @@
 
     seven = pl.ds(0, (GROUPS - 1) * TOK)
 
-    def scatter_done(h):
-        for kind in range(3):
-            await_bytes(o_out.at[h, seven, :], in_send.at[kind, h])
-
-    scatter_done(0)
+    def sent(kind, h):
+        await_bytes(o_out.at[h, seven, :], in_send.at[kind, h])
+
+    send_across(0)
+    for kind in range(3):
+        sent(kind, 0)
     scatter_k(1)
     scatter_v(1)
     scatter_q(1)
     send_own(0)
-    scatter_done(1)
-    scatter_k(2)
-    scatter_v(2)
-    scatter_q(2)
     before(0)
     score_step(0, 0, 0)
 
@@ -257,10 +273,26 @@
         score_step(p, 1, 1)
         value_step(p, 0, 0)
 
-        for h in range(1, HPG):
-            @pl.when(p == 2 * h - 1)
-            def _():
-                send_own(h)
+        @pl.when(p == 0)
+        def _():
+            sent(0, 1)
+            scatter_k(2)
+
+        @pl.when(p == 1)
+        def _():
+            sent(1, 1)
+            scatter_v(2)
+            sent(2, 1)
+            scatter_q(2)
+            send_own(1)
+            send_across(1)
+            forward_near(0)
+
+        @pl.when(p == 4)
+        def _():
+            send_own(2)
+            send_across(2)
+
         for at, h in FORWARD_NEAR.items():
             @pl.when(p == at)
             def _():
@@ -280,13 +312,15 @@
         value_step(p, 1, 1)
 
         for h in range(HPG):
-            @pl.when(p == 18 + h)
+            @pl.when(p == ORDER.index((h, 3, 1)))
             def _():
                 send_part(h)
 
-            @pl.when(p == 21 + h)
+        for h in range(HPG - 1):
+            @pl.when(p == ORDER.index((h, 3, 0)))
             def _():
                 send_result(h)
+
         return carry
 
     def score_step_next(p):
@@ -303,7 +337,8 @@
         await_bytes(o_out.at[h], o_recv.at[h])
     o_ref[...] = o_in[...]
 
-    scatter_done(2)
+    for kind in range(3):
+        sent(kind, 2)
     for h in range(HPG):
         await_bytes(o_out.at[h, seven, :], o_send.at[h])
         await_bytes(part_out.at[h], part_sem.at[0, h, 0])

time: 133 us -> 117 us (0.88)
  Pallas kernels: 131 us -> 115 us
    pallas_call x1, Pallas kernels: 131 us -> 115 us  [shards(): pl.pallas_call(kernel, out_shape=jax.ShapeDtypeStruct((TOK, width), bf16)...]
where the time goes in v3:
time: 117 us
  Pallas kernels  115 us (98%)
  local copies, waits for them, and re-layouts  2.06 us (2%)
    pallas_call x1, Pallas kernels, shards(): pl.pallas_call(kernel, out_shape=jax.ShapeDtypeStruct((TOK, width), bf16)...  115 us

profile of v3, /device:TPU:0, one launch (start us, length us, event | category | flops | bytes accessed | tf_op | source)
XLA Modules:
  0.0 117.0 jit_solution(1447852050232177491)
XLA Ops:
  0.0 114.9 %shard_map.55 = bf16[128,3072]{1,0:T(8,128)(2,1)} custom-call(bf16[128,3072]{1,0:T(8,128)(2,1)} %q_in.1, bf16[128,3072]{1,0:T(8,128)(2,1)} %k_in.1, bf16[128,3072]{1,0:T(8,128)(2,1)} %v_in.1, f32[1,3072]{1,0:T(1,128)} %bitcast.2, f32[1,3072]{1,0:T(1,128)} %bitcast.3), custom_call_target="tpu_custom_call" | custom-call | tf_op jit(solution)/shard_map/pallas_call | solution.py:361
  114.9 2.1 %copy.7 = bf16[128,3072]{1,0:T(8,128)(2,1)} copy(bf16[128,3072]{1,0:T(8,128)(2,1)} %shard_map.55) | data formatting | bytes 1572864

commit v4 on v3

--- a/solution.py
+++ b/solution.py
@@ -18,15 +18,16 @@
 KEYS = 2 * ROWS
 SCALE = math.log2(math.e) / math.sqrt(HEAD_DIM)
 MESH = pl.DeviceIdType.MESH
+PIECE = ROWS // 2
 ORDER = (
-    (0, 0, 0), (0, 0, 1), (1, 0, 0), (0, 1, 0), (0, 1, 1), (0, 2, 0),
-    (0, 2, 1), (1, 0, 1), (2, 0, 0), (1, 1, 0), (1, 1, 1), (1, 2, 0),
-    (1, 2, 1), (0, 3, 1), (2, 0, 1), (1, 3, 1), (2, 1, 0), (2, 1, 1),
-    (2, 2, 0), (2, 2, 1), (2, 3, 1), (0, 3, 0), (1, 3, 0), (2, 3, 0),
+    (0, 0, 0), (0, 1, 0), (0, 0, 1), (0, 2, 0), (0, 1, 1), (1, 0, 0),
+    (0, 2, 1), (1, 0, 1), (1, 1, 0), (0, 3, 1), (1, 1, 1), (1, 2, 0),
+    (1, 2, 1), (2, 0, 0), (2, 0, 1), (1, 3, 1), (2, 1, 0), (2, 1, 1),
+    (0, 3, 0), (2, 2, 1), (2, 3, 1), (1, 3, 0), (2, 2, 0), (2, 3, 0),
 )
 PAIRS = len(ORDER)
-FORWARD_NEAR = {7: 1, 11: 2}
-FORWARD_FAR = {8: 0, 12: 1, 17: 2}
+FORWARD_NEAR = {0: (0, 0), 2: (0, 1), 6: (1, 0), 9: (1, 1), 13: (2, 0), 15: (2, 1)}
+FORWARD_FAR = {7: 0, 13: 1, 17: 2}
 
 
 def first_uses(key):
@@ -133,23 +134,34 @@
     def scatter_q(h):
         scatter(qn, lambda r: q_all.at[h, 0, r, :], 2, q_recv.at[h, 0], h)
 
-    scatter_q(0)
     scatter_k(0)
     scatter_v(0)
+    scatter_q(0)
     acc[...] = jnp.zeros_like(acc)
     top[...] = jnp.full_like(top, -1e30)
 
+    def piece(t, h, slot, n):
+        rows = pl.ds(n * PIECE, PIECE)
+        if t == 0:
+            return k_all.at[h, slot, rows, :]
+        return v_all.at[h, slot, rows, pl.ds(0, HEAD_DIM)]
+
     def send_own(h):
-        await_bytes(k_chunk(h, 0, 0), kv_recv.at[0, h, 0, 0])
-        await_bytes(v_chunk(h, 0, 0), kv_recv.at[1, h, 0, 0])
+        def near(t, n):
+            mine = piece(t, h, 0, n)
+            remote(mine, piece(t, h, 1 + n, 0), kv_send.at[t, h, 0, 1],
+                   kv_recv.at[t, h, 1 + n, 0], above).start()
+            remote(mine, piece(t, h, 1 + n, 1), kv_send.at[t, h, 0, 2],
+                   kv_recv.at[t, h, 1 + n, 0], below).start()
+
         for t, chunk in ((0, k_chunk), (1, v_chunk)):
             mine = chunk(h, 0, 0)
+            await_bytes(mine, kv_recv.at[t, h, 0, 0])
+            near(t, 0)
             remote(mine, chunk(h, 0, 1), kv_send.at[t, h, 0, 0],
                    kv_recv.at[t, h, 0, 1], other_core).start()
-            remote(mine, chunk(h, 1, 0), kv_send.at[t, h, 0, 1],
-                   kv_recv.at[t, h, 1, 0], above).start()
-            remote(mine, chunk(h, 2, 0), kv_send.at[t, h, 0, 2],
-                   kv_recv.at[t, h, 2, 0], below).start()
+        near(0, 1)
+        near(1, 1)
 
     def send_across(h):
         await_bytes(q_all.at[h, 0], q_recv.at[h, 0])
@@ -161,17 +173,14 @@
         remote(chunk(h, slot, 0), chunk(h, slot, 1), kv_send.at[t, h, slot, 0],
                kv_recv.at[t, h, slot, 1], other_core).start()
 
-    def forward_near(h):
+    def forward_near(h, n):
         for t, chunk in ((0, k_chunk), (1, v_chunk)):
-            for slot in (1, 2):
-                await_bytes(chunk(h, slot, 0), kv_recv.at[t, h, slot, 0])
-        remote(k_chunk(h, 1, 0), k_chunk(h, 3, 0), kv_send.at[0, h, 1, 1],
+            await_bytes(chunk(h, 1 + n, 0), kv_recv.at[t, h, 1 + n, 0])
+            to_other_core(t, h, 1 + n)
+        remote(piece(0, h, 1 + n, 0), piece(0, h, 3, n), kv_send.at[0, h, 1, 1],
                kv_recv.at[0, h, 3, 0], above).start()
-        remote(v_chunk(h, 2, 0), v_chunk(h, 3, 0), kv_send.at[1, h, 2, 1],
+        remote(piece(1, h, 1 + n, 1), piece(1, h, 3, n), kv_send.at[1, h, 2, 1],
                kv_recv.at[1, h, 3, 0], below).start()
-        for slot in (1, 2):
-            for t in (0, 1):
-                to_other_core(t, h, slot)
 
     def forward_far(h):
         for t, chunk in ((0, k_chunk), (1, v_chunk)):
@@ -232,40 +241,48 @@
         remote(lse_out.at[h], lse_in.at[h], part_sem.at[0, h, 1],
                part_sem.at[1, h, 1], across).start()
 
-    def send_result(h):
-        await_bytes(part_in.at[h], part_sem.at[1, h, 0])
-        await_bytes(lse_in.at[h], part_sem.at[1, h, 1])
-        for block in range(ROWS // BQ):
-            rows = pl.ds(block * BQ, BQ)
-            mean, lse = finish_block(h, 0, block)
-            row = jnp.broadcast_to(lse_in[h, 0:1, rows], (HEAD_DIM, BQ))
-            lse2 = jnp.transpose(row)
-            high = jnp.maximum(lse, lse2)
-            w1 = jnp.exp2(lse - high)
-            w2 = jnp.exp2(lse2 - high)
-            both = mean * w1 + part_in[h, rows, :].astype(jnp.float32) * w2
-            o_out[h, rows, :] = (both / (w1 + w2)).astype(jnp.bfloat16)
+    def send_result(h, block):
+        if block == 0:
+            await_bytes(part_in.at[h], part_sem.at[1, h, 0])
+            await_bytes(lse_in.at[h], part_sem.at[1, h, 1])
+        rows = pl.ds(block * BQ, BQ)
+        mean, lse = finish_block(h, 0, block)
+        row = jnp.broadcast_to(lse_in[h, 0:1, rows], (HEAD_DIM, BQ))
+        lse2 = jnp.transpose(row)
+        high = jnp.maximum(lse, lse2)
+        w1 = jnp.exp2(lse - high)
+        w2 = jnp.exp2(lse2 - high)
+        both = mean * w1 + part_in[h, rows, :].astype(jnp.float32) * w2
+        o_out[h, rows, :] = (both / (w1 + w2)).astype(jnp.bfloat16)
         target = cols(c * HPG + h)
-        pltpu.make_async_copy(
-            o_out.at[h, rows_of(c), :], o_in.at[:, target], o_recv.at[h]
-        ).start()
-        for d in range(1, GROUPS):
-            g = (c + d) % GROUPS
-            remote(o_out.at[h, rows_of(g), :], o_in.at[:, target],
-                   o_send.at[h], o_recv.at[h], (b, g)).start()
+        for g in range(block * BQ // TOK, (block + 1) * BQ // TOK):
+            @pl.when(g == c)
+            def _():
+                pltpu.make_async_copy(
+                    o_out.at[h, rows_of(c), :], o_in.at[:, target], o_recv.at[h]
+                ).start()
+
+            @pl.when(g != c)
+            def _():
+                remote(o_out.at[h, rows_of(g), :], o_in.at[:, target],
+                       o_send.at[h], o_recv.at[h], (b, g)).start()
 
     seven = pl.ds(0, (GROUPS - 1) * TOK)
 
     def sent(kind, h):
         await_bytes(o_out.at[h, seven, :], in_send.at[kind, h])
 
+    send_own(0)
+    sent(0, 0)
+    sent(1, 0)
+    scatter_k(1)
     send_across(0)
-    for kind in range(3):
-        sent(kind, 0)
-    scatter_k(1)
+    sent(2, 0)
     scatter_v(1)
     scatter_q(1)
-    send_own(0)
+    scatter_k(2)
+    scatter_v(2)
+    scatter_q(2)
     before(0)
     score_step(0, 0, 0)
 
@@ -273,30 +290,21 @@
         score_step(p, 1, 1)
         value_step(p, 0, 0)
 
-        @pl.when(p == 0)
+        for at, (h, n) in FORWARD_NEAR.items():
+            @pl.when(p == at)
+            def _():
+                forward_near(h, n)
+
+        @pl.when(p == 3)
         def _():
-            sent(0, 1)
-            scatter_k(2)
-
-        @pl.when(p == 1)
-        def _():
-            sent(1, 1)
-            scatter_v(2)
-            sent(2, 1)
-            scatter_q(2)
             send_own(1)
             send_across(1)
-            forward_near(0)
-
-        @pl.when(p == 4)
+
+        @pl.when(p == 8)
         def _():
             send_own(2)
             send_across(2)
 
-        for at, h in FORWARD_NEAR.items():
-            @pl.when(p == at)
-            def _():
-                forward_near(h)
         for at, h in FORWARD_FAR.items():
             @pl.when(p == at)
             def _():
@@ -319,7 +327,8 @@
         for h in range(HPG - 1):
             @pl.when(p == ORDER.index((h, 3, 0)))
             def _():
-                send_result(h)
+                send_result(h, 0)
+                send_result(h, 1)
 
         return carry
 
@@ -330,14 +339,16 @@
     p = PAIRS - 1
     score_step(p, 1, 1)
     value_step(p, 0, 0)
+    send_result(HPG - 1, 0)
     value_step(p, 1, 1)
-    send_result(HPG - 1)
+    send_result(HPG - 1, 1)
 
     for h in range(HPG):
         await_bytes(o_out.at[h], o_recv.at[h])
     o_ref[...] = o_in[...]
 
     for kind in range(3):
+        sent(kind, 1)
         sent(kind, 2)
     for h in range(HPG):
         await_bytes(o_out.at[h, seven, :], o_send.at[h])

time: 117 us -> 114 us (0.974)
  Pallas kernels: 115 us -> 112 us
    pallas_call x1, Pallas kernels: 115 us -> 112 us  [shards(): pl.pallas_call(kernel, out_shape=jax.ShapeDtypeStruct((TOK, width), bf16)...]
where the time goes in v4:
time: 114 us
  Pallas kernels  112 us (98%)
  local copies, waits for them, and re-layouts  2.06 us (2%)
    pallas_call x1, Pallas kernels, shards(): pl.pallas_call(kernel, out_shape=jax.ShapeDtypeStruct((TOK, width), bf16)...  112 us

profile of v4, /device:TPU:0, one launch (start us, length us, event | category | flops | bytes accessed | tf_op | source)
XLA Modules:
  0.0 113.7 jit_solution(2617055283917022205)
XLA Ops:
  0.0 111.6 %shard_map.55 = bf16[128,3072]{1,0:T(8,128)(2,1)} custom-call(bf16[128,3072]{1,0:T(8,128)(2,1)} %q_in.1, bf16[128,3072]{1,0:T(8,128)(2,1)} %k_in.1, bf16[128,3072]{1,0:T(8,128)(2,1)} %v_in.1, f32[1,3072]{1,0:T(1,128)} %bitcast.2, f32[1,3072]{1,0:T(1,128)} %bitcast.3), custom_call_target="tpu_custom_call" | custom-call | tf_op jit(solution)/shard_map/pallas_call | solution.py:372
  111.6 2.1 %copy.7 = bf16[128,3072]{1,0:T(8,128)(2,1)} copy(bf16[128,3072]{1,0:T(8,128)(2,1)} %shard_map.55) | data formatting | bytes 1572864

commit v5 on v4

--- a/solution.py
+++ b/solution.py
@@ -280,15 +280,18 @@
     sent(2, 0)
     scatter_v(1)
     scatter_q(1)
-    scatter_k(2)
-    scatter_v(2)
-    scatter_q(2)
     before(0)
     score_step(0, 0, 0)
 
     def pair(p, carry):
         score_step(p, 1, 1)
         value_step(p, 0, 0)
+
+        @pl.when(p == 0)
+        def _():
+            scatter_k(2)
+            scatter_v(2)
+            scatter_q(2)
 
         for at, (h, n) in FORWARD_NEAR.items():
             @pl.when(p == at)

time: 114 us -> 114 us (level)
  no operation moved by 1% of the time
where the time goes in v5:
time: 114 us
  Pallas kernels  111 us (97%)
  local copies, waits for them, and re-layouts  2.06 us (2%)
    pallas_call x1, Pallas kernels, shards(): pl.pallas_call(kernel, out_shape=jax.ShapeDtypeStruct((TOK, width), bf16)...  111 us

profile of v5, /device:TPU:0, one launch (start us, length us, event | category | flops | bytes accessed | tf_op | source)
XLA Modules:
  0.0 113.5 jit_solution(9753627311844074163)
XLA Ops:
  0.0 111.5 %shard_map.55 = bf16[128,3072]{1,0:T(8,128)(2,1)} custom-call(bf16[128,3072]{1,0:T(8,128)(2,1)} %q_in.1, bf16[128,3072]{1,0:T(8,128)(2,1)} %k_in.1, bf16[128,3072]{1,0:T(8,128)(2,1)} %v_in.1, f32[1,3072]{1,0:T(1,128)} %bitcast.2, f32[1,3072]{1,0:T(1,128)} %bitcast.3), custom_call_target="tpu_custom_call" | custom-call | tf_op jit(solution)/shard_map/pallas_call | solution.py:375
  111.5 2.1 %copy.7 = bf16[128,3072]{1,0:T(8,128)(2,1)} copy(bf16[128,3072]{1,0:T(8,128)(2,1)} %shard_map.55) | data formatting | bytes 1572864
